TPU v7x, 512 devices: a whole 4x4x16 slice. The times are simulated.
512 devices in a mesh: grp: 16 (over x_lo, y, core), dev: 32 (over x_hi, z).
Axes of the slice: x: 4 (x_hi: 2, x_lo: 2; x = x_hi * 2 + x_lo), y: 4, z: 16, core: 2. Of those that a mesh axis runs over, the one named last changes fastest.
Arguments:
- voltage: float32 [2, 4096, 4192], P(None, ('grp', 'dev')), may hold values from -6 to 6
- filter_taps: float32 [4, 32], replicated, may hold values from -0.5 to 0.5
- plan: int32 [16, 9], P('grp'), may hold values from 0 to 8, each once within a row
Outputs:
- visibility: bfloat16 [16, 9, 32, 2, 256, 256], P('grp', None, 'dev')
Inputs may be any that keep to these rules, and one draw needn't show every extreme that they name: Each row of plan holds every distance 0 to 8 once.
All inputs are finite; a program needn't handle non-finite values.
Results may differ from a plain program's by a relative error of at most 0.0056.
Values may be sent and summed in bfloat16 or wider, within the bound.
No kernel may reach another device: no remote copies, remote signals or barrier semaphores. Data moves between devices by JAX's collectives and lax.ppermute only.
A program may use at most 64 MiB of HBM per device.

v0:
```python
import math
import jax
import jax.numpy as jnp
from jax import lax
from jax.sharding import PartitionSpec as P

F = 32
TAPS = 4
SPECTRA = 128
FRAMES = 131


def shifted(x, axis, by):
    length = lax.axis_size(axis)
    return lax.ppermute(x, axis, [(i, (i + by) % length) for i in range(length)])


def compute_spectra(voltage, filter_taps):
    signal_input_count = voltage.shape[1]
    framed_samples = voltage.reshape(2, signal_input_count, FRAMES, F)
    filtered = filter_taps[0][None, None, None, :] * framed_samples[:, :, 0:SPECTRA, :]
    for p in range(1, TAPS):
        filtered = (
            filtered
            + filter_taps[p][None, None, None, :] * framed_samples[:, :, p : p + SPECTRA, :]
        )
    indices = jnp.arange(F, dtype=jnp.int32)
    phase_angle = (indices[:, None] * indices[None, :] % F).astype(jnp.float32) * (
        2.0 * math.pi / F
    )
    cosine_table = jnp.cos(phase_angle)
    sine_table = jnp.sin(phase_angle)
    highest = lax.Precision.HIGHEST
    real_part = jnp.einsum(
        "csn,nf->fcs", filtered[0], cosine_table, precision=highest
    ) + jnp.einsum("csn,nf->fcs", filtered[1], sine_table, precision=highest)
    imaginary_component = jnp.einsum(
        "csn,nf->fcs", filtered[1], cosine_table, precision=highest
    ) - jnp.einsum("csn,nf->fcs", filtered[0], sine_table, precision=highest)
    return jnp.stack([real_part, imaginary_component], axis=2).astype(jnp.bfloat16)


def correlate(own_block, partner):
    chans, rows_here = (own_block.shape[0], own_block.shape[1])
    left_spectrum_rows = own_block.reshape(chans, rows_here, -1)
    real_part = partner[:, :, 0, :]
    imaginary_component = partner[:, :, 1, :]
    right_spectrum_rows = jnp.stack(
        [
            jnp.concatenate([real_part, imaginary_component], -1),
            jnp.concatenate([-imaginary_component, real_part], -1),
        ],
        axis=1,
    )
    cross_products = jnp.einsum(
        "gzi,gkvi->gkzv",
        left_spectrum_rows,
        right_spectrum_rows,
        preferred_element_type=jnp.float32,
    )
    return (cross_products / SPECTRA).astype(jnp.bfloat16)


def per_device(voltage, filter_taps, plan):
    local_spectra = compute_spectra(voltage, filter_taps)
    own_block = lax.all_to_all(local_spectra, "dev", split_axis=0, concat_axis=1, tiled=True)
    groups = lax.axis_size("grp")
    rounds = groups // 2 + 1
    results = [correlate(own_block, own_block)]
    received = own_block
    for distance in range(1, rounds):
        received = shifted(own_block, "grp", distance)
        results.append(correlate(own_block, received))
    stacked = jnp.stack(results, axis=0)
    return jnp.take(stacked, plan[0], axis=0)[None]


def solution(mesh):
    return jax.shard_map(
        per_device,
        mesh=mesh,
        in_specs=(P(None, ("grp", "dev"), None), P(), P("grp", None)),
        out_specs=P("grp", None, "dev", None, None, None),
        check_vma=False,
    )
```

profile of v0, /device:TPU:1, one launch (start us, length us, event | category | flops | bytes accessed | tf_op | source)
XLA Modules:
  0.0 89.8 jit_solution(14616734474427329352)
XLA Ops:
  0.0 1.3 %reshape.257 = f32[2,8,131,32]{3,2,1,0:T(8,128)S(1)} reshape(f32[2,8,4192]{2,1,0:T(8,128)} %param.3) | data formatting | bytes 536576 | tf_op jit(solution)/shard_map/reshape | solution.py:20
  1.3 1.8 %fusion.111 = (f32[2,8,128,32]{3,2,1,0:T(8,128)S(1)}, f32[2,8,128,32]{3,2,1,0:T(8,128)}, f32[2,8,128,32]{3,2,1,0:T(8,128)S(1)}, f32[2,8,128,32]{3,2,1,0:T(8,128)}) fusion(f32[2,8,131,32]{3,2,1,0:T(8,128)S(1)} %reshape.257), kind=kLoop, calls=%fused_computation.181 | loop fusion | bytes 2097152 | tf_op jit(solution)/shard_map/slice | solution.py:21
  3.1 1.5 %copy.22 = f32[2,8,128,32]{2,3,1,0:T(8,128)S(1)} copy(f32[2,8,128,32]{3,2,1,0:T(8,128)} %get-tuple-element.8) | data formatting | bytes 524288
  4.6 1.5 %copy.21 = f32[2,8,128,32]{2,3,1,0:T(8,128)S(1)} copy(f32[2,8,128,32]{3,2,1,0:T(8,128)} %get-tuple-element.6) | data formatting | bytes 524288
  6.2 0.3 copy.20
  6.5 0.3 copy.19
  7.0 0.3 fusion.59
  7.3 0.3 fusion.58
  7.7 0.3 fusion.29
  8.0 0.3 fusion.30
  8.4 0.7 copy.16
  9.1 18.5 %all-to-all-start = ((bf16[32,8,2,128]{3,1,2,0:T(8,128)(2,1)}), bf16[32,8,2,128]{3,1,2,0:T(8,128)(2,1)S(1)}, u32[]{:S(2)}, u32[]{:S(2)}) async-start(bf16[32,8,2,128]{3,1,2,0:T(8,128)(2,1)} %copy.16), calls=%async_computation | async-start | bytes 262144 | tf_op jit(solution)/shard_map/all_to_all | solution.py:66
  27.6 16.3 %all-to-all-done = bf16[32,8,2,128]{3,1,2,0:T(8,128)(2,1)S(1)} async-done(((bf16[32,8,2,128]{3,1,2,0:T(8,128)(2,1)}), bf16[32,8,2,128]{3,1,2,0:T(8,128)(2,1)S(1)}, u32[]{:S(2)}, u32[]{:S(2)}) %all-to-all-start) | async-done | bytes 131104 | tf_op jit(solution)/shard_map/all_to_all | solution.py:66
  44.0 6.1 %collective-permute-start = (bf16[1,256,2,128]{3,1,2,0:T(8,128)(2,1)S(1)}, bf16[1,256,2,128]{3,1,2,0:T(8,128)(2,1)S(1)}, u32[]{:S(2)}, u32[]{:S(2)}) collective-permute-start(bf16[1,256,2,128]{3,1,2,0:T(8,128)(2,1)S(1)} %bitcast.255), channel_id=1, source_target_pairs={{0,32},{32,64},{64,96},{96,128},{128,160},{160,192},{192,224},{224... | collective-permute-start | bytes 393224 | tf_op jit(solution)/shard_map/ppermute | solution.py:15
  50.1 3.2 %collective-permute-start.1 = (bf16[1,256,2,128]{3,1,2,0:T(8,128)(2,1)S(1)}, bf16[1,256,2,128]{3,1,2,0:T(8,128)(2,1)S(1)}, u32[]{:S(2)}, u32[]{:S(2)}) collective-permute-start(bf16[1,256,2,128]{3,1,2,0:T(8,128)(2,1)S(1)} %bitcast.256), channel_id=1, source_target_pairs={{0,64},{32,96},{64,128},{96,160},{128,192},{160,224},{192,256},{22... | collective-permute-start | bytes 393224 | tf_op jit(solution)/shard_map/ppermute | solution.py:15
  53.3 3.5 %collective-permute-start.2 = (bf16[1,256,2,128]{3,1,2,0:T(8,128)(2,1)S(1)}, bf16[1,256,2,128]{3,1,2,0:T(8,128)(2,1)S(1)}, u32[]{:S(2)}, u32[]{:S(2)}) collective-permute-start(bf16[1,256,2,128]{3,1,2,0:T(8,128)(2,1)S(1)} %bitcast.257), channel_id=1, source_target_pairs={{0,96},{32,128},{64,160},{96,192},{128,224},{160,256},{192,288},{2... | collective-permute-start | bytes 393224 | tf_op jit(solution)/shard_map/ppermute | solution.py:15
  56.8 2.3 %collective-permute-start.3 = (bf16[1,256,2,128]{3,1,2,0:T(8,128)(2,1)S(1)}, bf16[1,256,2,128]{3,1,2,0:T(8,128)(2,1)S(1)}, u32[]{:S(2)}, u32[]{:S(2)}) collective-permute-start(bf16[1,256,2,128]{3,1,2,0:T(8,128)(2,1)S(1)} %bitcast.258), channel_id=1, source_target_pairs={{0,128},{32,160},{64,192},{96,224},{128,256},{160,288},{192,320},{... | collective-permute-start | bytes 393224 | tf_op jit(solution)/shard_map/ppermute | solution.py:15
  59.1 4.7 %collective-permute-start.4 = (bf16[1,256,2,128]{3,1,2,0:T(8,128)(2,1)S(1)}, bf16[1,256,2,128]{3,1,2,0:T(8,128)(2,1)S(1)}, u32[]{:S(2)}, u32[]{:S(2)}) collective-permute-start(bf16[1,256,2,128]{3,1,2,0:T(8,128)(2,1)S(1)} %bitcast.259), channel_id=1, source_target_pairs={{0,160},{32,192},{64,224},{96,256},{128,288},{160,320},{192,352},{... | collective-permute-start | bytes 393224 | tf_op jit(solution)/shard_map/ppermute | solution.py:15
  64.1 2.8 %collective-permute-start.5 = (bf16[1,256,2,128]{3,1,2,0:T(8,128)(2,1)S(1)}, bf16[1,256,2,128]{3,1,2,0:T(8,128)(2,1)S(1)}, u32[]{:S(2)}, u32[]{:S(2)}) collective-permute-start(bf16[1,256,2,128]{3,1,2,0:T(8,128)(2,1)S(1)} %bitcast.260), channel_id=1, source_target_pairs={{0,192},{32,224},{64,256},{96,288},{128,320},{160,352},{192,384},{... | collective-permute-start | bytes 393224 | tf_op jit(solution)/shard_map/ppermute | solution.py:15
  67.0 3.6 %collective-permute-start.6 = (bf16[1,256,2,128]{3,1,2,0:T(8,128)(2,1)S(1)}, bf16[1,256,2,128]{3,1,2,0:T(8,128)(2,1)S(1)}, u32[]{:S(2)}, u32[]{:S(2)}) collective-permute-start(bf16[1,256,2,128]{3,1,2,0:T(8,128)(2,1)S(1)} %bitcast.261), channel_id=1, source_target_pairs={{0,224},{32,256},{64,288},{96,320},{128,352},{160,384},{192,416},{... | collective-permute-start | bytes 393224 | tf_op jit(solution)/shard_map/ppermute | solution.py:15
  70.7 3.1 %collective-permute-start.7 = (bf16[1,256,2,128]{3,1,2,0:T(8,128)(2,1)S(1)}, bf16[1,256,2,128]{3,1,2,0:T(8,128)(2,1)S(1)}, u32[]{:S(2)}, u32[]{:S(2)}) collective-permute-start(bf16[1,256,2,128]{3,1,2,0:T(8,128)(2,1)S(1)} %bitcast.262), channel_id=1, source_target_pairs={{0,256},{32,288},{64,320},{96,352},{128,384},{160,416},{192,448},{... | collective-permute-start | bytes 393224 | tf_op jit(solution)/shard_map/ppermute | solution.py:15
  74.1 1.4 %collective-permute-done.6 = bf16[1,256,2,128]{3,1,2,0:T(8,128)(2,1)S(1)} collective-permute-done((bf16[1,256,2,128]{3,1,2,0:T(8,128)(2,1)S(1)}, bf16[1,256,2,128]{3,1,2,0:T(8,128)(2,1)S(1)}, u32[]{:S(2)}, u32[]{:S(2)}) %collective-permute-start.6) | collective-permute-done | bytes 131104 | tf_op jit(solution)/shard_map/ppermute | solution.py:15
  75.7 2.2 %collective-permute-done.7 = bf16[1,256,2,128]{3,1,2,0:T(8,128)(2,1)S(1)} collective-permute-done((bf16[1,256,2,128]{3,1,2,0:T(8,128)(2,1)S(1)}, bf16[1,256,2,128]{3,1,2,0:T(8,128)(2,1)S(1)}, u32[]{:S(2)}, u32[]{:S(2)}) %collective-permute-start.7) | collective-permute-done | bytes 131104 | tf_op jit(solution)/shard_map/ppermute | solution.py:15
  78.2 0.3 fusion.22
  78.4 0.3 fusion.20
  78.7 0.3 fusion.18
  79.0 0.3 fusion.16
  79.2 0.3 fusion.14
  80.1 1.4 %copy-done = bf16[9,1,2,256,256]{3,4,2,1,0:T(8,128)(2,1)} copy-done((bf16[9,1,2,256,256]{3,4,2,1,0:T(8,128)(2,1)}, bf16[9,1,2,256,256]{3,4,2,1,0:T(8,128)(2,1)S(1)}, u32[]{:S(2)}) %copy-start) | copy-done | bytes 2359320
  81.5 2.4 %gather_fusion = bf16[9,2,256,256]{2,3,1,0:T(8,128)(2,1)S(1)} fusion(bf16[9,2,256,256]{2,3,1,0:T(8,128)(2,1)} %bitcast.252, s32[1024]{0:T(1024)S(1)} %pad_clamp_fusion), kind=kCustom, calls=%fused_computation | custom fusion | bytes 4718628 | tf_op jit(solution)/shard_map/jit(_take)/gather | solution.py:75
  83.8 1.7 %bitcast_select_fusion = bf16[1,9,1,2,256,256]{4,5,3,1,2,0:T(8,128)(2,1)} fusion(bf16[9,2,256,256]{2,3,1,0:T(8,128)(2,1)S(1)} %gather_fusion, pred[9]{0:T(512)(128)(4,1)S(1)} %compare_and_fusion), kind=kLoop, calls=%fused_computation.1 | loop fusion | flops 1179648 | bytes 4718601 | tf_op jit(solution)/shard_map/jit(_take)/select_n | solution.py:75
  85.5 4.3 %copy.18 = bf16[1,9,1,2,256,256]{5,4,3,2,1,0:T(8,128)(2,1)} copy(bf16[1,9,1,2,256,256]{4,5,3,1,2,0:T(8,128)(2,1)} %bitcast_select_fusion) | data formatting | bytes 4718592 | tf_op jit(solution)/shard_map/jit(_take)/select_n | solution.py:75
  (49 shorter events, 1.7 us)
Async XLA Ops:
  3.1 3.7 %copy-start.1 = (f32[4,32]{1,0:T(4,128)S(1)}, f32[4,32]{1,0:T(4,128)}, u32[]{:S(2)}) copy-start(f32[4,32]{1,0:T(4,128)} %param.4) | copy-start | bytes 1540
  6.5 21.1 %copy-start.2 = (s32[1,9]{1,0:T(1,128)S(1)}, s32[1,9]{1,0:T(1,128)}, u32[]{:S(2)}) copy-start(s32[1,9]{1,0:T(1,128)} %param.5) | copy-start | bytes 112
  9.1 34.8 %all-to-all-start = ((bf16[32,8,2,128]{3,1,2,0:T(8,128)(2,1)}), bf16[32,8,2,128]{3,1,2,0:T(8,128)(2,1)S(1)}, u32[]{:S(2)}, u32[]{:S(2)}) async-start(bf16[32,8,2,128]{3,1,2,0:T(8,128)(2,1)} %copy.16), calls=%async_computation | async-start | bytes 262144 | tf_op jit(solution)/shard_map/all_to_all | solution.py:66
  44.0 20.2 %collective-permute-start = (bf16[1,256,2,128]{3,1,2,0:T(8,128)(2,1)S(1)}, bf16[1,256,2,128]{3,1,2,0:T(8,128)(2,1)S(1)}, u32[]{:S(2)}, u32[]{:S(2)}) collective-permute-start(bf16[1,256,2,128]{3,1,2,0:T(8,128)(2,1)S(1)} %bitcast.255), channel_id=1, source_target_pairs={{0,32},{32,64},{64,96},{96,128},{128,160},{160,192},{192,224},{224... | collective-permute-start | bytes 393224 | tf_op jit(solution)/shard_map/ppermute | solution.py:15
  50.1 17.0 %collective-permute-start.1 = (bf16[1,256,2,128]{3,1,2,0:T(8,128)(2,1)S(1)}, bf16[1,256,2,128]{3,1,2,0:T(8,128)(2,1)S(1)}, u32[]{:S(2)}, u32[]{:S(2)}) collective-permute-start(bf16[1,256,2,128]{3,1,2,0:T(8,128)(2,1)S(1)} %bitcast.256), channel_id=1, source_target_pairs={{0,64},{32,96},{64,128},{96,160},{128,192},{160,224},{192,256},{22... | collective-permute-start | bytes 393224 | tf_op jit(solution)/shard_map/ppermute | solution.py:15
  53.3 17.4 %collective-permute-start.2 = (bf16[1,256,2,128]{3,1,2,0:T(8,128)(2,1)S(1)}, bf16[1,256,2,128]{3,1,2,0:T(8,128)(2,1)S(1)}, u32[]{:S(2)}, u32[]{:S(2)}) collective-permute-start(bf16[1,256,2,128]{3,1,2,0:T(8,128)(2,1)S(1)} %bitcast.257), channel_id=1, source_target_pairs={{0,96},{32,128},{64,160},{96,192},{128,224},{160,256},{192,288},{2... | collective-permute-start | bytes 393224 | tf_op jit(solution)/shard_map/ppermute | solution.py:15
  56.8 17.0 %collective-permute-start.3 = (bf16[1,256,2,128]{3,1,2,0:T(8,128)(2,1)S(1)}, bf16[1,256,2,128]{3,1,2,0:T(8,128)(2,1)S(1)}, u32[]{:S(2)}, u32[]{:S(2)}) collective-permute-start(bf16[1,256,2,128]{3,1,2,0:T(8,128)(2,1)S(1)} %bitcast.258), channel_id=1, source_target_pairs={{0,128},{32,160},{64,192},{96,224},{128,256},{160,288},{192,320},{... | collective-permute-start | bytes 393224 | tf_op jit(solution)/shard_map/ppermute | solution.py:15
  59.1 14.8 %collective-permute-start.4 = (bf16[1,256,2,128]{3,1,2,0:T(8,128)(2,1)S(1)}, bf16[1,256,2,128]{3,1,2,0:T(8,128)(2,1)S(1)}, u32[]{:S(2)}, u32[]{:S(2)}) collective-permute-start(bf16[1,256,2,128]{3,1,2,0:T(8,128)(2,1)S(1)} %bitcast.259), channel_id=1, source_target_pairs={{0,160},{32,192},{64,224},{96,256},{128,288},{160,320},{192,352},{... | collective-permute-start | bytes 393224 | tf_op jit(solution)/shard_map/ppermute | solution.py:15
  64.1 9.9 %collective-permute-start.5 = (bf16[1,256,2,128]{3,1,2,0:T(8,128)(2,1)S(1)}, bf16[1,256,2,128]{3,1,2,0:T(8,128)(2,1)S(1)}, u32[]{:S(2)}, u32[]{:S(2)}) collective-permute-start(bf16[1,256,2,128]{3,1,2,0:T(8,128)(2,1)S(1)} %bitcast.260), channel_id=1, source_target_pairs={{0,192},{32,224},{64,256},{96,288},{128,320},{160,352},{192,384},{... | collective-permute-start | bytes 393224 | tf_op jit(solution)/shard_map/ppermute | solution.py:15
  67.0 8.5 %collective-permute-start.6 = (bf16[1,256,2,128]{3,1,2,0:T(8,128)(2,1)S(1)}, bf16[1,256,2,128]{3,1,2,0:T(8,128)(2,1)S(1)}, u32[]{:S(2)}, u32[]{:S(2)}) collective-permute-start(bf16[1,256,2,128]{3,1,2,0:T(8,128)(2,1)S(1)} %bitcast.261), channel_id=1, source_target_pairs={{0,224},{32,256},{64,288},{96,320},{128,352},{160,384},{192,416},{... | collective-permute-start | bytes 393224 | tf_op jit(solution)/shard_map/ppermute | solution.py:15
  70.7 7.1 %collective-permute-start.7 = (bf16[1,256,2,128]{3,1,2,0:T(8,128)(2,1)S(1)}, bf16[1,256,2,128]{3,1,2,0:T(8,128)(2,1)S(1)}, u32[]{:S(2)}, u32[]{:S(2)}) collective-permute-start(bf16[1,256,2,128]{3,1,2,0:T(8,128)(2,1)S(1)} %bitcast.262), channel_id=1, source_target_pairs={{0,256},{32,288},{64,320},{96,352},{128,384},{160,416},{192,448},{... | collective-permute-start | bytes 393224 | tf_op jit(solution)/shard_map/ppermute | solution.py:15
  80.0 1.4 %copy-start = (bf16[9,1,2,256,256]{3,4,2,1,0:T(8,128)(2,1)}, bf16[9,1,2,256,256]{3,4,2,1,0:T(8,128)(2,1)S(1)}, u32[]{:S(2)}) copy-start(bf16[9,1,2,256,256]{3,4,2,1,0:T(8,128)(2,1)S(1)} %fusion.10) | copy-start | bytes 7077892
where the time goes:
time: 90.4 us; the launch traced here: 89.8 us
  starting transfers between devices  47.8 us (53%)
  waiting for transfers between devices  19.9 us (22%)
  local copies, waits for them, and re-layouts  15.6 us (17%)
  matrix products  3.73 us (4%)
  other arithmetic  2.26 us (2%)
    ppermute x8, starting transfers between devices, shifted(): lax.ppermute(x, axis, [(i, (i + by) % length) for i in range(length)])  29.3 us
    all_to_all x1, starting transfers between devices, per_device(): lax.all_to_all(local_spectra, 'dev', split_axis=0, concat_axis=1, tiled=T...  18.5 us
    all_to_all x1, waiting for transfers between devices, per_device(): lax.all_to_all(local_spectra, 'dev', split_axis=0, concat_axis=1, tiled=T...  16.3 us
    unnamed x10, local copies, waits for them, and re-layouts  5.1 us
    select_n x1, local copies, waits for them, and re-layouts, per_device(): return jnp.take(stacked, plan[0], axis=0)[None]  4.26 us
    ppermute x8, waiting for transfers between devices, shifted(): lax.ppermute(x, axis, [(i, (i + by) % length) for i in range(length)])  3.6 us
    gather x1, local copies, waits for them, and re-layouts, per_device(): return jnp.take(stacked, plan[0], axis=0)[None]  2.36 us
    dot_general x9, matrix products, correlate(): jnp.einsum('gzi,gkvi->gkzv', left_spectrum_rows, right_spectrum_rows, pre...  2.35 us
  transfers between devices with their start and end apart: 9, of which 3 were waited for; matrix products, arithmetic and copies ran while one was open for 1% of the time, Pallas kernels for 0%

commit v1 on v0

--- a/solution.py
+++ b/solution.py
@@ -63,7 +63,12 @@
 
 def per_device(voltage, filter_taps, plan):
     local_spectra = compute_spectra(voltage, filter_taps)
-    own_block = lax.all_to_all(local_spectra, "dev", split_axis=0, concat_axis=1, tiled=True)
+    own_block = jnp.concatenate(
+        lax.all_to_all(
+            jnp.stack(jnp.split(local_spectra, lax.axis_size("dev"), axis=0)), "dev", 0, 0
+        ),
+        axis=1,
+    )
     groups = lax.axis_size("grp")
     rounds = groups // 2 + 1
     results = [correlate(own_block, own_block)]

time: 90.4 us -> 106 us (1.17)
  local copies, waits for them, and re-layouts: 15.6 us -> 29.3 us
  matrix products: 3.73 us -> 5.17 us
    unnamed x10 -> x35, local copies, waits for them, and re-layouts: 5.1 us -> 19.8 us
    slice x1 -> x0, local copies, waits for them, and re-layouts: 1.77 us -> none  [compute_spectra(): framed_samples[:, :, 0:SPECTRA, :]]
where the time goes in v1:
time: 106 us
  starting transfers between devices  47.8 us (45%)
  local copies, waits for them, and re-layouts  29.3 us (28%)
  waiting for transfers between devices  19.9 us (19%)
  matrix products  5.17 us (5%)
  other arithmetic  2.88 us (3%)
    ppermute x8, starting transfers between devices, shifted(): lax.ppermute(x, axis, [(i, (i + by) % length) for i in range(length)])  29.3 us
    unnamed x35, local copies, waits for them, and re-layouts  19.8 us
    all_to_all x1, starting transfers between devices, per_device(): lax.all_to_all(jnp.stack(jnp.split(local_spectra, lax.axis_size('dev'), a...  18.5 us
    all_to_all x1, waiting for transfers between devices, per_device(): lax.all_to_all(jnp.stack(jnp.split(local_spectra, lax.axis_size('dev'), a...  16.3 us
    select_n x1, local copies, waits for them, and re-layouts, per_device(): return jnp.take(stacked, plan[0], axis=0)[None]  4.26 us
    ppermute x8, waiting for transfers between devices, shifted(): lax.ppermute(x, axis, [(i, (i + by) % length) for i in range(length)])  3.61 us
    gather x1, local copies, waits for them, and re-layouts, per_device(): return jnp.take(stacked, plan[0], axis=0)[None]  2.36 us
    dot_general x9, matrix products, correlate(): jnp.einsum('gzi,gkvi->gkzv', left_spectrum_rows, right_spectrum_rows, pre...  2.36 us
  transfers between devices with their start and end apart: 9, of which 3 were waited for; matrix products, arithmetic and copies ran while one was open for 1% of the time, Pallas kernels for 0%

profile of v1, /device:TPU:1, one launch (start us, length us, event | category | flops | bytes accessed | tf_op | source)
XLA Modules:
  0.0 105.5 jit_solution(4229521097712392980)
XLA Ops:
  0.0 1.3 %reshape.247 = f32[2,8,131,32]{3,2,1,0:T(8,128)S(1)} reshape(f32[2,8,4192]{2,1,0:T(8,128)} %param.3) | data formatting | bytes 536576 | tf_op jit(solution)/shard_map/reshape | solution.py:20
  1.3 0.8 slice_bitcast_fusion.27
  2.6 0.7 fusion.35
  3.3 0.7 fusion.34
  4.0 0.7 fusion.29
  4.7 0.7 fusion.30
  5.8 0.6 constant_dynamic-update-slice_fusion.31
  6.4 0.6 constant_dynamic-update-slice_fusion.30
  8.8 0.6 constant_dynamic-update-slice_fusion.26
  9.4 0.6 constant_dynamic-update-slice_fusion.25
  10.0 0.6 constant_dynamic-update-slice_fusion.24
  12.3 0.6 constant_dynamic-update-slice_fusion.20
  12.9 0.6 constant_dynamic-update-slice_fusion.19
  13.5 0.6 constant_dynamic-update-slice_fusion.18
  14.1 0.6 constant_dynamic-update-slice_fusion.17
  16.5 0.6 constant_dynamic-update-slice_fusion.13
  24.8 18.5 %all-to-all-start = ((bf16[32,1,8,2,128]{4,2,3,1,0:T(8,128)(2,1)}), bf16[32,1,8,2,128]{4,2,3,1,0:T(8,128)(2,1)S(1)}, u32[]{:S(2)}, u32[]{:S(2)}) async-start(bf16[32,1,8,2,128]{4,2,3,1,0:T(8,128)(2,1)} %constant_dynamic-update-slice_fusion), calls=%async_computation | async-start | bytes 262144 | tf_op jit(solution)/shard_map/all_to_all | solution.py:67
  43.4 16.3 %all-to-all-done = bf16[32,1,8,2,128]{4,2,3,1,0:T(8,128)(2,1)S(1)} async-done(((bf16[32,1,8,2,128]{4,2,3,1,0:T(8,128)(2,1)}), bf16[32,1,8,2,128]{4,2,3,1,0:T(8,128)(2,1)S(1)}, u32[]{:S(2)}, u32[]{:S(2)}) %all-to-all-start) | async-done | bytes 131104 | tf_op jit(solution)/shard_map/all_to_all | solution.py:67
  59.7 6.1 %collective-permute-start = (bf16[1,256,2,128]{3,1,2,0:T(8,128)(2,1)S(1)}, bf16[1,256,2,128]{3,1,2,0:T(8,128)(2,1)S(1)}, u32[]{:S(2)}, u32[]{:S(2)}) collective-permute-start(bf16[1,256,2,128]{3,1,2,0:T(8,128)(2,1)S(1)} %bitcast.323), channel_id=1, source_target_pairs={{0,32},{32,64},{64,96},{96,128},{128,160},{160,192},{192,224},{224... | collective-permute-start | bytes 393224 | tf_op jit(solution)/shard_map/ppermute | solution.py:15
  65.8 3.2 %collective-permute-start.1 = (bf16[1,256,2,128]{3,1,2,0:T(8,128)(2,1)S(1)}, bf16[1,256,2,128]{3,1,2,0:T(8,128)(2,1)S(1)}, u32[]{:S(2)}, u32[]{:S(2)}) collective-permute-start(bf16[1,256,2,128]{3,1,2,0:T(8,128)(2,1)S(1)} %bitcast.324), channel_id=1, source_target_pairs={{0,64},{32,96},{64,128},{96,160},{128,192},{160,224},{192,256},{22... | collective-permute-start | bytes 393224 | tf_op jit(solution)/shard_map/ppermute | solution.py:15
  69.0 3.5 %collective-permute-start.2 = (bf16[1,256,2,128]{3,1,2,0:T(8,128)(2,1)S(1)}, bf16[1,256,2,128]{3,1,2,0:T(8,128)(2,1)S(1)}, u32[]{:S(2)}, u32[]{:S(2)}) collective-permute-start(bf16[1,256,2,128]{3,1,2,0:T(8,128)(2,1)S(1)} %bitcast.325), channel_id=1, source_target_pairs={{0,96},{32,128},{64,160},{96,192},{128,224},{160,256},{192,288},{2... | collective-permute-start | bytes 393224 | tf_op jit(solution)/shard_map/ppermute | solution.py:15
  72.5 2.3 %collective-permute-start.3 = (bf16[1,256,2,128]{3,1,2,0:T(8,128)(2,1)S(1)}, bf16[1,256,2,128]{3,1,2,0:T(8,128)(2,1)S(1)}, u32[]{:S(2)}, u32[]{:S(2)}) collective-permute-start(bf16[1,256,2,128]{3,1,2,0:T(8,128)(2,1)S(1)} %bitcast.326), channel_id=1, source_target_pairs={{0,128},{32,160},{64,192},{96,224},{128,256},{160,288},{192,320},{... | collective-permute-start | bytes 393224 | tf_op jit(solution)/shard_map/ppermute | solution.py:15
  74.8 4.7 %collective-permute-start.4 = (bf16[1,256,2,128]{3,1,2,0:T(8,128)(2,1)S(1)}, bf16[1,256,2,128]{3,1,2,0:T(8,128)(2,1)S(1)}, u32[]{:S(2)}, u32[]{:S(2)}) collective-permute-start(bf16[1,256,2,128]{3,1,2,0:T(8,128)(2,1)S(1)} %bitcast.327), channel_id=1, source_target_pairs={{0,160},{32,192},{64,224},{96,256},{128,288},{160,320},{192,352},{... | collective-permute-start | bytes 393224 | tf_op jit(solution)/shard_map/ppermute | solution.py:15
  79.8 2.8 %collective-permute-start.5 = (bf16[1,256,2,128]{3,1,2,0:T(8,128)(2,1)S(1)}, bf16[1,256,2,128]{3,1,2,0:T(8,128)(2,1)S(1)}, u32[]{:S(2)}, u32[]{:S(2)}) collective-permute-start(bf16[1,256,2,128]{3,1,2,0:T(8,128)(2,1)S(1)} %bitcast.328), channel_id=1, source_target_pairs={{0,192},{32,224},{64,256},{96,288},{128,320},{160,352},{192,384},{... | collective-permute-start | bytes 393224 | tf_op jit(solution)/shard_map/ppermute | solution.py:15
  82.7 3.6 %collective-permute-start.6 = (bf16[1,256,2,128]{3,1,2,0:T(8,128)(2,1)S(1)}, bf16[1,256,2,128]{3,1,2,0:T(8,128)(2,1)S(1)}, u32[]{:S(2)}, u32[]{:S(2)}) collective-permute-start(bf16[1,256,2,128]{3,1,2,0:T(8,128)(2,1)S(1)} %bitcast.329), channel_id=1, source_target_pairs={{0,224},{32,256},{64,288},{96,320},{128,352},{160,384},{192,416},{... | collective-permute-start | bytes 393224 | tf_op jit(solution)/shard_map/ppermute | solution.py:15
  86.4 3.1 %collective-permute-start.7 = (bf16[1,256,2,128]{3,1,2,0:T(8,128)(2,1)S(1)}, bf16[1,256,2,128]{3,1,2,0:T(8,128)(2,1)S(1)}, u32[]{:S(2)}, u32[]{:S(2)}) collective-permute-start(bf16[1,256,2,128]{3,1,2,0:T(8,128)(2,1)S(1)} %bitcast.330), channel_id=1, source_target_pairs={{0,256},{32,288},{64,320},{96,352},{128,384},{160,416},{192,448},{... | collective-permute-start | bytes 393224 | tf_op jit(solution)/shard_map/ppermute | solution.py:15
  89.9 1.4 %collective-permute-done.6 = bf16[1,256,2,128]{3,1,2,0:T(8,128)(2,1)S(1)} collective-permute-done((bf16[1,256,2,128]{3,1,2,0:T(8,128)(2,1)S(1)}, bf16[1,256,2,128]{3,1,2,0:T(8,128)(2,1)S(1)}, u32[]{:S(2)}, u32[]{:S(2)}) %collective-permute-start.6) | collective-permute-done | bytes 131104 | tf_op jit(solution)/shard_map/ppermute | solution.py:15
  91.4 2.2 %collective-permute-done.7 = bf16[1,256,2,128]{3,1,2,0:T(8,128)(2,1)S(1)} collective-permute-done((bf16[1,256,2,128]{3,1,2,0:T(8,128)(2,1)S(1)}, bf16[1,256,2,128]{3,1,2,0:T(8,128)(2,1)S(1)}, u32[]{:S(2)}, u32[]{:S(2)}) %collective-permute-start.7) | collective-permute-done | bytes 131104 | tf_op jit(solution)/shard_map/ppermute | solution.py:15
  95.8 1.4 %copy-done = bf16[9,1,2,256,256]{3,4,2,1,0:T(8,128)(2,1)} copy-done((bf16[9,1,2,256,256]{3,4,2,1,0:T(8,128)(2,1)}, bf16[9,1,2,256,256]{3,4,2,1,0:T(8,128)(2,1)S(1)}, u32[]{:S(2)}) %copy-start) | copy-done | bytes 2359320
  97.2 2.4 %gather_fusion = bf16[9,2,256,256]{2,3,1,0:T(8,128)(2,1)S(1)} fusion(bf16[9,2,256,256]{2,3,1,0:T(8,128)(2,1)} %bitcast.320, s32[1024]{0:T(1024)S(1)} %pad_clamp_fusion), kind=kCustom, calls=%fused_computation | custom fusion | bytes 4718628 | tf_op jit(solution)/shard_map/jit(_take)/gather | solution.py:80
  99.6 1.7 %bitcast_select_fusion = bf16[1,9,1,2,256,256]{4,5,3,1,2,0:T(8,128)(2,1)} fusion(bf16[9,2,256,256]{2,3,1,0:T(8,128)(2,1)S(1)} %gather_fusion, pred[9]{0:T(512)(128)(4,1)S(1)} %compare_and_fusion), kind=kLoop, calls=%fused_computation.1 | loop fusion | flops 1179648 | bytes 4718601 | tf_op jit(solution)/shard_map/jit(_take)/select_n | solution.py:80
  101.3 4.3 %copy.684 = bf16[1,9,1,2,256,256]{5,4,3,2,1,0:T(8,128)(2,1)} copy(bf16[1,9,1,2,256,256]{4,5,3,1,2,0:T(8,128)(2,1)} %bitcast_select_fusion) | data formatting | bytes 4718592 | tf_op jit(solution)/shard_map/jit(_take)/select_n | solution.py:80
  (76 shorter events, 16.7 us)
Async XLA Ops:
  2.6 40.7 %copy-start.1 = (s32[1,9]{1,0:T(1,128)S(1)}, s32[1,9]{1,0:T(1,128)}, u32[]{:S(2)}) copy-start(s32[1,9]{1,0:T(1,128)} %param.5) | copy-start | bytes 112
  24.8 34.8 %all-to-all-start = ((bf16[32,1,8,2,128]{4,2,3,1,0:T(8,128)(2,1)}), bf16[32,1,8,2,128]{4,2,3,1,0:T(8,128)(2,1)S(1)}, u32[]{:S(2)}, u32[]{:S(2)}) async-start(bf16[32,1,8,2,128]{4,2,3,1,0:T(8,128)(2,1)} %constant_dynamic-update-slice_fusion), calls=%async_computation | async-start | bytes 262144 | tf_op jit(solution)/shard_map/all_to_all | solution.py:67
  59.7 20.2 %collective-permute-start = (bf16[1,256,2,128]{3,1,2,0:T(8,128)(2,1)S(1)}, bf16[1,256,2,128]{3,1,2,0:T(8,128)(2,1)S(1)}, u32[]{:S(2)}, u32[]{:S(2)}) collective-permute-start(bf16[1,256,2,128]{3,1,2,0:T(8,128)(2,1)S(1)} %bitcast.323), channel_id=1, source_target_pairs={{0,32},{32,64},{64,96},{96,128},{128,160},{160,192},{192,224},{224... | collective-permute-start | bytes 393224 | tf_op jit(solution)/shard_map/ppermute | solution.py:15
  65.8 16.9 %collective-permute-start.1 = (bf16[1,256,2,128]{3,1,2,0:T(8,128)(2,1)S(1)}, bf16[1,256,2,128]{3,1,2,0:T(8,128)(2,1)S(1)}, u32[]{:S(2)}, u32[]{:S(2)}) collective-permute-start(bf16[1,256,2,128]{3,1,2,0:T(8,128)(2,1)S(1)} %bitcast.324), channel_id=1, source_target_pairs={{0,64},{32,96},{64,128},{96,160},{128,192},{160,224},{192,256},{22... | collective-permute-start | bytes 393224 | tf_op jit(solution)/shard_map/ppermute | solution.py:15
  69.0 17.4 %collective-permute-start.2 = (bf16[1,256,2,128]{3,1,2,0:T(8,128)(2,1)S(1)}, bf16[1,256,2,128]{3,1,2,0:T(8,128)(2,1)S(1)}, u32[]{:S(2)}, u32[]{:S(2)}) collective-permute-start(bf16[1,256,2,128]{3,1,2,0:T(8,128)(2,1)S(1)} %bitcast.325), channel_id=1, source_target_pairs={{0,96},{32,128},{64,160},{96,192},{128,224},{160,256},{192,288},{2... | collective-permute-start | bytes 393224 | tf_op jit(solution)/shard_map/ppermute | solution.py:15
  72.5 17.0 %collective-permute-start.3 = (bf16[1,256,2,128]{3,1,2,0:T(8,128)(2,1)S(1)}, bf16[1,256,2,128]{3,1,2,0:T(8,128)(2,1)S(1)}, u32[]{:S(2)}, u32[]{:S(2)}) collective-permute-start(bf16[1,256,2,128]{3,1,2,0:T(8,128)(2,1)S(1)} %bitcast.326), channel_id=1, source_target_pairs={{0,128},{32,160},{64,192},{96,224},{128,256},{160,288},{192,320},{... | collective-permute-start | bytes 393224 | tf_op jit(solution)/shard_map/ppermute | solution.py:15
  74.8 14.8 %collective-permute-start.4 = (bf16[1,256,2,128]{3,1,2,0:T(8,128)(2,1)S(1)}, bf16[1,256,2,128]{3,1,2,0:T(8,128)(2,1)S(1)}, u32[]{:S(2)}, u32[]{:S(2)}) collective-permute-start(bf16[1,256,2,128]{3,1,2,0:T(8,128)(2,1)S(1)} %bitcast.327), channel_id=1, source_target_pairs={{0,160},{32,192},{64,224},{96,256},{128,288},{160,320},{192,352},{... | collective-permute-start | bytes 393224 | tf_op jit(solution)/shard_map/ppermute | solution.py:15
  79.8 9.9 %collective-permute-start.5 = (bf16[1,256,2,128]{3,1,2,0:T(8,128)(2,1)S(1)}, bf16[1,256,2,128]{3,1,2,0:T(8,128)(2,1)S(1)}, u32[]{:S(2)}, u32[]{:S(2)}) collective-permute-start(bf16[1,256,2,128]{3,1,2,0:T(8,128)(2,1)S(1)} %bitcast.328), channel_id=1, source_target_pairs={{0,192},{32,224},{64,256},{96,288},{128,320},{160,352},{192,384},{... | collective-permute-start | bytes 393224 | tf_op jit(solution)/shard_map/ppermute | solution.py:15
  82.7 8.5 %collective-permute-start.6 = (bf16[1,256,2,128]{3,1,2,0:T(8,128)(2,1)S(1)}, bf16[1,256,2,128]{3,1,2,0:T(8,128)(2,1)S(1)}, u32[]{:S(2)}, u32[]{:S(2)}) collective-permute-start(bf16[1,256,2,128]{3,1,2,0:T(8,128)(2,1)S(1)} %bitcast.329), channel_id=1, source_target_pairs={{0,224},{32,256},{64,288},{96,320},{128,352},{160,384},{192,416},{... | collective-permute-start | bytes 393224 | tf_op jit(solution)/shard_map/ppermute | solution.py:15
  86.4 7.1 %collective-permute-start.7 = (bf16[1,256,2,128]{3,1,2,0:T(8,128)(2,1)S(1)}, bf16[1,256,2,128]{3,1,2,0:T(8,128)(2,1)S(1)}, u32[]{:S(2)}, u32[]{:S(2)}) collective-permute-start(bf16[1,256,2,128]{3,1,2,0:T(8,128)(2,1)S(1)} %bitcast.330), channel_id=1, source_target_pairs={{0,256},{32,288},{64,320},{96,352},{128,384},{160,416},{192,448},{... | collective-permute-start | bytes 393224 | tf_op jit(solution)/shard_map/ppermute | solution.py:15
  95.8 1.4 %copy-start = (bf16[9,1,2,256,256]{3,4,2,1,0:T(8,128)(2,1)}, bf16[9,1,2,256,256]{3,4,2,1,0:T(8,128)(2,1)S(1)}, u32[]{:S(2)}) copy-start(bf16[9,1,2,256,256]{3,4,2,1,0:T(8,128)(2,1)S(1)} %fusion.10) | copy-start | bytes 7077892
